TPU v7x, 32 devices: a whole 2x2x4 slice. The times are simulated.
32 devices in a mesh: ab: 4 (over y, x), cd: 4 (over z), ij: 2 (over core).
Axes of the slice: x: 2, y: 2, z: 4, core: 2. Of those that a mesh axis runs over, the one named last changes fastest.
Arguments:
- amplitudes: float32 [512, 4096], P('ij', ('cd', 'ab')), may hold values from -6 to 6
- integrals: float32 [256, 256, 256], P(('ab', 'cd')), may hold values from -0.375 to 0.375
- tile_row: int32 [256], P(('ab', 'cd')), may hold values from 0 to 3, as said below
- tile_col: int32 [256], P(('ab', 'cd')), may hold values from 0 to 3
- tile_count: int32 [16], P(('ab', 'cd')), may hold values from 1 to 16, as said below
Outputs:
- residual: float32 [512, 4, 16, 64], P('ij', 'ab', 'cd')
Inputs may be any that keep to these rules, and one draw needn't show every extreme that they name: Within one slab the 16 slots name distinct (tile_row, tile_col) pairs. `tile_count`: in every draw some slab has all 16 slots live.
All inputs are finite; a program needn't handle non-finite values.
Results may differ from a plain program's by a relative error of at most 0.0003.
Values sent between devices are 32-bit elements; how exact they have to be, the bound alone decides.
A program may use at most 128 MiB of HBM per device.

v0:
```python
import math

import jax
import jax.numpy as jnp
from jax import lax
from jax.sharding import PartitionSpec as P


def from_partner(block, axis, bit):
    count = lax.axis_size(axis)
    route = []
    for low in range(count):
        high = low | 1 << bit
        if high != low and high < count:
            route += [(low, high), (high, low)]
    return lax.ppermute(block, axis, route)


def place_rows(chosen, tile_rows, row_picks, block_size):
    terms = jnp.einsum("okf,kef->oke", chosen, tile_rows, precision=lax.Precision.HIGHEST)
    occ_dev, slots, width = terms.shape
    terms = terms.reshape(occ_dev, slots, width // block_size, block_size)
    placed = jnp.einsum("rk,okab->aorb", row_picks, terms, precision=lax.Precision.HIGHEST)
    return placed.reshape(width // block_size, occ_dev, row_picks.shape[0] * block_size)


def per_device(amplitudes, integrals, tile_row, tile_col, tile_count):
    occ_dev = amplitudes.shape[0]
    slots = integrals.shape[0]
    tile_size = integrals.shape[1]
    block_size = math.isqrt(tile_size)
    blocks = lax.axis_size("ab")
    cd_size = lax.axis_size("cd")
    group_size = block_size // cd_size
    live_count = tile_count[0]
    live = jnp.arange(slots, dtype=jnp.int32) < live_count
    row_picks = (
        (tile_row[None, :] == jnp.arange(blocks, dtype=jnp.int32)[:, None]) & live[None, :]
    ).astype(jnp.float32)
    gathered = lax.all_gather(amplitudes, "ab", axis=1, tiled=True)
    columns = gathered.reshape(occ_dev, -1, tile_size)
    chosen = jnp.take(columns, tile_col, axis=1)
    partial_value = place_rows(chosen, integrals, row_picks, block_size)
    summed = lax.psum_scatter(partial_value, "cd", scatter_dimension=0, tiled=True)
    direct = jnp.transpose(summed, (1, 0, 2))
    outgoing = summed.reshape(group_size, occ_dev, blocks, cd_size, group_size)
    outgoing = jnp.transpose(outgoing, (2, 3, 1, 0, 4))
    arrived = lax.all_to_all(
        outgoing.reshape(blocks * cd_size, occ_dev * group_size * group_size),
        ("ab", "cd"),
        split_axis=0,
        concat_axis=0,
        tiled=True,
    )
    arrived = arrived.reshape(blocks, cd_size, occ_dev, group_size, group_size)
    mirrored = jnp.transpose(arrived, (2, 4, 0, 1, 3)).reshape(
        occ_dev, group_size, blocks * block_size
    )
    partner = from_partner(mirrored, "ij", 0)
    return (direct + partner).reshape(occ_dev, 1, group_size, blocks * block_size)


def solution(mesh):
    in_specs = (
        P("ij", ("cd", "ab")),
        P(("ab", "cd"), None, None),
        P(("ab", "cd")),
        P(("ab", "cd")),
        P(("ab", "cd")),
    )
    out_specs = P("ij", "ab", "cd", None)
    return jax.shard_map(
        per_device, mesh=mesh, in_specs=in_specs, out_specs=out_specs, check_vma=False
    )
```

profile of v0, /device:TPU:1, one launch (start us, length us, event | category | flops | bytes accessed | tf_op | source)
XLA Modules:
  0.0 149.5 jit_solution(6584111835509438171)
XLA Ops:
  6.5 0.0 all-gather.2.cloned.1.call-start
  6.5 1.8 %copy.17 = f32[256,256]{0,1:T(8,128)} copy(f32[256,256]{1,0:T(8,128)} %param.5) | data formatting | bytes 524288 | tf_op args[0]
  8.3 0.0 all-gather.2.cloned.1.call-update
  8.3 0.0 reduce-scatter.2.cloned.1.call-start
  9.1 0.7 compare_select_fusion
  9.7 0.7 compare_and_fusion
  10.4 27.2 %all-gather.2.cloned.1.call-done = f32[256,1024]{0,1:T(8,128)} async-done(((f32[256,256]{0,1:T(8,128)}), f32[256,1024]{0,1:T(8,128)}) %all-gather.2.cloned.1.call-update) | async-done | bytes 1048592 | tf_op jit(solution)/shard_map/all_gather | solution.py:40
  37.6 1.6 %copy.18 = f32[256,4,256]{2,0,1:T(8,128)S(1)} copy(f32[256,4,256]{0,2,1:T(8,128)} %bitcast.34) | data formatting | bytes 2097152 | tf_op jit(solution)/shard_map/reshape | solution.py:41
  39.2 2.8 %gather_fusion = f32[16,256,256]{2,1,0:T(8,128)} fusion(f32[256,4,256]{2,0,1:T(8,128)S(1)} %copy.18, s32[1024]{0:T(1024)S(1)} %pad_clamp_fusion), kind=kCustom, calls=%fused_computation | custom fusion | bytes 8388672 | tf_op jit(solution)/shard_map/jit(_take)/gather | solution.py:42
  41.9 0.0 copy-start.1
  41.9 12.3 %fusion = f32[16,256,256]{1,2,0:T(8,128)S(1)} fusion(f32[16,256,256]{2,1,0:T(8,128)} %param.6, f32[16,256,256]{2,1,0:T(8,128)} %gather_fusion, pred[16]{0:T(512)(128)(4,1)S(1)} %compare_and_fusion), kind=kOutput, calls=%fused_computation.1 | convolution fusion | flops 3222274048 | bytes 12582928 | tf_op jit(solution)/shard_map/okf,kef->oke/dot_general | solution.py:20
  54.2 0.0 copy-done.1
  54.2 3.9 %fusion.7 = f32[16,256,4,16]{1,2,3,0:T(4,128)S(1)} fusion(f32[256,16,16,16]{0,3,2,1:T(8,128)S(1)} %bitcast.32, s32[16]{0:T(128)S(1)} %copy-done.1, pred[16]{0:T(512)(128)(4,1)S(1)} %iota_compare_fusion.1), kind=kOutput, calls=%fused_computation.8 | convolution fusion | flops 50331776 | bytes 5242960 | tf_op jit(solution)/shard_map/rk,okab->aorb/dot_general | solution.py:23
  58.1 1.2 copy.20
  59.3 0.0 reduce-scatter.2.cloned.1.call-update
  59.3 27.2 %reduce-scatter.2.cloned.1.call-done = f32[4,256,64]{1,2,0:T(8,128)} async-done(((f32[16,256,64]{1,2,0:T(8,128)}), f32[4,256,64]{1,2,0:T(8,128)}) %reduce-scatter.2.cloned.1.call-update) | async-done | bytes 262160 | tf_op jit(solution)/shard_map/reduce_scatter | solution.py:44
  86.5 1.0 reshape.39
  87.5 5.9 %copy.21 = f32[4,256,4,4,4]{4,0,1,3,2:T(4,128)} copy(f32[4,256,4,4,4]{1,4,3,2,0:T(4,128)S(1)} %reshape.39) | data formatting | bytes 524288 | tf_op jit(solution)/shard_map/reshape | solution.py:46
  93.4 11.3 %all_to_all.8 = f32[16,1,4096]{2,1,0:T(1,128)S(1)} reshape(f32[4,4,256,4,4]{4,3,2,1,0:T(4,128)} %bitcast.30) | data formatting | bytes 524288 | tf_op jit(solution)/shard_map/all_to_all | solution.py:48
  104.7 13.3 %all_to_all.10 = f32[16,1,4096]{2,1,0:T(1,128)S(1)} all-to-all(f32[16,1,4096]{2,1,0:T(1,128)S(1)} %all_to_all.8), channel_id=1, replica_groups=mesh['ab'=4,'cd'=4,'ij'=2] {'ab','cd'}, dimensions={0} | all-to-all | bytes 524288 | tf_op jit(solution)/shard_map/all_to_all | solution.py:48
  118.0 0.6 reduce
  118.7 12.9 %reshape.40 = f32[4,4,256,4,4]{4,3,2,1,0:T(4,128)} reshape(f32[16,4096]{1,0:T(8,128)S(1)} %reduce) | data formatting | bytes 524288 | tf_op jit(solution)/shard_map/reshape | solution.py:55
  131.5 0.0 copy-start
  131.5 6.9 %copy.23 = f32[256,4,4,4,4]{0,4,3,2,1:T(4,128)S(1)} copy(f32[256,4,4,4,4]{1,4,0,3,2:T(4,128)} %bitcast.31) | data formatting | bytes 524288 | tf_op jit(solution)/shard_map/transpose | solution.py:56
  138.4 0.1 reshape.41
  138.5 2.3 %collective-permute-start = (f32[256,4,64]{0,2,1:T(8,128)S(1)}, f32[256,4,64]{0,2,1:T(8,128)S(1)}, u32[]{:S(2)}, u32[]{:S(2)}) collective-permute-start(f32[256,4,64]{0,2,1:T(8,128)S(1)} %reshape.41), channel_id=1, source_target_pairs={{0,1},{1,0},{2,3},{3,2},{4,5},{5,4},{6,7},{7,6},{8,9},{9,8},{10,11... | collective-permute-start | bytes 786440 | tf_op jit(solution)/shard_map/ppermute | solution.py:16
  140.8 1.2 collective-permute-done
  141.9 0.0 copy-done
  141.9 0.7 fusion.10
  (2 shorter events, 0.0 us)
Async XLA Ops:
  6.5 31.1 %all-gather.2.cloned.1.call-start = ((), (), s32[]{:S(2)}) async-start(), calls=%async_computation.2 | async-start | bytes 1310720 | tf_op jit(solution)/shard_map/all_gather | solution.py:40
  8.3 78.2 %reduce-scatter.2.cloned.1.call-start = ((), (), s32[]{:S(2)}) async-start(), calls=%async_computation.3 | async-start | bytes 1310720 | tf_op jit(solution)/shard_map/reduce_scatter | solution.py:44
  41.9 12.3 %copy-start.1 = (s32[16]{0:T(128)S(1)}, s32[16]{0:T(128)}, u32[]{:S(2)}) copy-start(s32[16]{0:T(128)} %param.7) | copy-start | bytes 196
  131.5 10.4 %copy-start = (f32[4,256,64]{1,2,0:T(8,128)S(1)}, f32[4,256,64]{1,2,0:T(8,128)}, u32[]{:S(2)}) copy-start(f32[4,256,64]{1,2,0:T(8,128)} %reduce-scatter.2.cloned.1.call-done) | copy-start | bytes 786436
  138.5 3.4 %collective-permute-start = (f32[256,4,64]{0,2,1:T(8,128)S(1)}, f32[256,4,64]{0,2,1:T(8,128)S(1)}, u32[]{:S(2)}, u32[]{:S(2)}) collective-permute-start(f32[256,4,64]{0,2,1:T(8,128)S(1)} %reshape.41), channel_id=1, source_target_pairs={{0,1},{1,0},{2,3},{3,2},{4,5},{5,4},{6,7},{7,6},{8,9},{9,8},{10,11... | collective-permute-start | bytes 786440 | tf_op jit(solution)/shard_map/ppermute | solution.py:16
Sparse Core Ops, SparseCore 0:
  9.2 28.3 all-gather.1
  59.4 27.0 reduce-scatter.1
where the time goes:
time: 150 us
  waiting for transfers between devices  55.6 us (37%)
  local copies, waits for them, and re-layouts  45.3 us (30%)
  matrix products  16.2 us (11%)
  between operations  14.1 us (9%)
  blocking collectives  13.3 us (9%)
  other arithmetic  2.69 us (2%)
  starting transfers between devices  2.32 us (2%)
    all_gather x1, waiting for transfers between devices, per_device(): gathered = lax.all_gather(amplitudes, 'ab', axis=1, tiled=True)  27.2 us
    reduce_scatter x1, waiting for transfers between devices, per_device(): lax.psum_scatter(partial_value, 'cd', scatter_dimension=0, tiled=True)  27.2 us
    all_to_all x1, blocking collectives, per_device(): lax.all_to_all(outgoing.reshape(blocks * cd_size, occ_dev * group_size *...  13.3 us
    reshape x1, local copies, waits for them, and re-layouts, per_device(): arrived = arrived.reshape(blocks, cd_size, occ_dev, group_size, group_size)  12.9 us
    dot_general x1, matrix products, place_rows(): jnp.einsum('okf,kef->oke', chosen, tile_rows, precision=lax.Precision.HIG...  12.3 us
    all_to_all x1, local copies, waits for them, and re-layouts, per_device(): lax.all_to_all(outgoing.reshape(blocks * cd_size, occ_dev * group_size *...  11.3 us
    reshape x2, local copies, waits for them, and re-layouts, per_device(): outgoing = summed.reshape(group_size, occ_dev, blocks, cd_size, group_size)  6.91 us
    transpose x1, local copies, waits for them, and re-layouts, per_device(): jnp.transpose(arrived, (2, 4, 0, 1, 3))  6.88 us
  transfers between devices with their start and end apart: 3, of which 3 were waited for; matrix products, arithmetic and copies ran while one was open for 1% of the time, Pallas kernels for 0%

commit v1 on v0

--- a/solution.py
+++ b/solution.py
@@ -1,9 +1,218 @@
+import functools
 import math
 
 import jax
 import jax.numpy as jnp
 from jax import lax
+from jax.experimental import pallas as pl
+from jax.experimental.pallas import tpu as pltpu
 from jax.sharding import PartitionSpec as P
+
+MESH = pl.DeviceIdType.MESH
+LANES = 128
+
+
+def split(value):
+    high = value.astype(jnp.bfloat16)
+    low = (value - high.astype(jnp.float32)).astype(jnp.bfloat16)
+    return high, low
+
+
+def ladder_kernel(
+    n_ab, n_cd, block, chunks,
+    row_ref, col_ref, count_ref, amp_ref, tiles_ref, out_ref,
+    tiles, w_high, w_low, gathered, a_high, a_low, partial, arrived, summed, outgoing, mirrored,
+    tile_sem, own_sem, ag_send, ag_recv, rs_send, rs_recv, mi_send, mi_recv,
+):
+    me_ab, me_cd, me_ij = lax.axis_index("ab"), lax.axis_index("cd"), lax.axis_index("ij")
+    slots, size = tiles_ref.shape[0], tiles_ref.shape[1]
+    group = block // n_cd
+    rows = group * n_ab * block
+    targets = n_ab * n_cd
+    piece = group * group
+    own_place = me_ab * n_cd + me_cd
+
+    tile_copies = [
+        pltpu.make_async_copy(tiles_ref.at[k], tiles.at[k], tile_sem.at[k]) for k in range(slots)
+    ]
+    for copy in tile_copies:
+        copy.start()
+    own = pltpu.make_async_copy(amp_ref, gathered.at[0], own_sem)
+    own.start()
+
+    barrier = pltpu.get_barrier_semaphore()
+    for j in range(1, n_ab):
+        pl.semaphore_signal(
+            barrier, inc=1, device_id=(lax.rem(me_ab + j, n_ab), me_cd, me_ij), device_id_type=MESH
+        )
+    for i in range(1, n_cd):
+        pl.semaphore_signal(
+            barrier, inc=1, device_id=(me_ab, lax.rem(me_cd + i, n_cd), me_ij), device_id_type=MESH
+        )
+    for p in range(n_ab):
+        for q in range(n_cd):
+            pl.semaphore_signal(barrier, inc=1, device_id=(p, q, 1 - me_ij), device_id_type=MESH)
+    pl.semaphore_wait(barrier, n_ab - 1 + n_cd - 1 + targets)
+
+    ag = {}
+    for h in range(chunks):
+        part = pl.ds(h * LANES, LANES)
+        for j in range(1, n_ab):
+            ag[h, j] = pltpu.make_async_remote_copy(
+                src_ref=amp_ref.at[part],
+                dst_ref=gathered.at[j, part],
+                send_sem=ag_send.at[h, j],
+                recv_sem=ag_recv.at[h, j],
+                device_id=(lax.rem(me_ab + j, n_ab), me_cd, me_ij),
+                device_id_type=MESH,
+            )
+            ag[h, j].start()
+
+    keys = [row_ref[k] * n_ab + col_ref[k] for k in range(slots)]
+    live_count = count_ref[0]
+    for copy in tile_copies:
+        copy.wait()
+    for j in range(n_ab):
+        column = lax.rem(me_ab - j + n_ab, n_ab)
+        for r in range(n_ab):
+            slot = jnp.int32(0)
+            for k in range(1, slots):
+                slot = jnp.where(keys[k] == r * n_ab + column, jnp.int32(k), slot)
+            scale = jnp.where(slot < live_count, jnp.float32(1), jnp.float32(0))
+            high, low = split(tiles[slot] * scale)
+            at = (slice(None), pl.ds(r * block, block), pl.ds(j * size, size))
+            w_high[at] = high.reshape(block, block, size)
+            w_low[at] = low.reshape(block, block, size)
+
+    own.wait()
+    rs = {}
+    mi = {}
+    contract = (((1,), (1,)), ((), ()))
+
+    def finish(h):
+        for i in range(1, n_cd):
+            rs[h, i].wait_recv()
+        total = partial[h, 0]
+        for i in range(1, n_cd):
+            total = total + arrived[h, i]
+        summed[h] = total
+        for x in range(group):
+            for y in range(group):
+                outgoing[h, pl.ds(x * group + y, targets, stride=piece), :] = summed[
+                    h, pl.ds(x * n_ab * block + y, targets, stride=group), :
+                ]
+        for p in range(n_ab):
+            for q in range(n_cd):
+                t = p * n_cd + q
+                mi[h, t] = pltpu.make_async_remote_copy(
+                    src_ref=outgoing.at[h, pl.ds(t * piece, piece)],
+                    dst_ref=mirrored.at[h, pl.ds(own_place * piece, piece)],
+                    send_sem=mi_send.at[h, t],
+                    recv_sem=mi_recv.at[h, own_place],
+                    device_id=(p, q, 1 - me_ij),
+                    device_id_type=MESH,
+                )
+                mi[h, t].start()
+
+    for h in range(chunks):
+        part = pl.ds(h * LANES, LANES)
+        for j in range(n_ab):
+            if j:
+                ag[h, j].wait_recv()
+            high, low = split(gathered[j, part])
+            a_high[:, pl.ds(j * size, size)] = high
+            a_low[:, pl.ds(j * size, size)] = low
+        for i in [*range(1, n_cd), 0]:
+            d = lax.rem(me_cd + i, n_cd)
+            lead = pl.ds(d * group, group)
+            left_high = w_high[lead].reshape(rows, n_ab * size)
+            left_low = w_low[lead].reshape(rows, n_ab * size)
+            right_high, right_low = a_high[...], a_low[...]
+            value = lax.dot_general(
+                left_high, right_low, contract, preferred_element_type=jnp.float32
+            )
+            value += lax.dot_general(
+                left_low, right_high, contract, preferred_element_type=jnp.float32
+            )
+            value += lax.dot_general(
+                left_high, right_high, contract, preferred_element_type=jnp.float32
+            )
+            partial[h, i] = value
+            if i:
+                rs[h, i] = pltpu.make_async_remote_copy(
+                    src_ref=partial.at[h, i],
+                    dst_ref=arrived.at[h, i],
+                    send_sem=rs_send.at[h, i],
+                    recv_sem=rs_recv.at[h, i],
+                    device_id=(me_ab, d, me_ij),
+                    device_id_type=MESH,
+                )
+                rs[h, i].start()
+    for h in range(chunks):
+        finish(h)
+    for h in range(chunks):
+        for s in range(targets):
+            pltpu.make_async_remote_copy(
+                src_ref=outgoing.at[h, pl.ds(s * piece, piece)],
+                dst_ref=mirrored.at[h, pl.ds(s * piece, piece)],
+                send_sem=mi_send.at[h, s],
+                recv_sem=mi_recv.at[h, s],
+                device_id=(me_ab, me_cd, 1 - me_ij),
+                device_id_type=MESH,
+            ).wait_recv()
+        for y in range(group):
+            out_ref[y, :, pl.ds(h * LANES, LANES)] = (
+                summed[h, pl.ds(y * n_ab * block, n_ab * block), :]
+                + mirrored[h, pl.ds(y, targets * group, stride=group), :]
+            )
+    for copy in [*ag.values(), *rs.values(), *mi.values()]:
+        copy.wait_send()
+
+
+def fused(amplitudes, integrals, tile_row, tile_col, tile_count):
+    occ_dev = amplitudes.shape[0]
+    slots, size = integrals.shape[0], integrals.shape[1]
+    block = math.isqrt(size)
+    n_ab, n_cd = lax.axis_size("ab"), lax.axis_size("cd")
+    group = block // n_cd
+    rows = group * n_ab * block
+    chunks = occ_dev // LANES
+    targets = n_ab * n_cd
+    piece = group * group
+    f32, bf16 = jnp.float32, jnp.bfloat16
+    dma = pltpu.SemaphoreType.DMA
+    out = pl.pallas_call(
+        functools.partial(ladder_kernel, n_ab, n_cd, block, chunks),
+        out_shape=jax.ShapeDtypeStruct((group, n_ab * block, occ_dev), f32),
+        in_specs=[pl.BlockSpec(memory_space=pltpu.SMEM)] * 3
+        + [pl.BlockSpec(memory_space=pl.ANY)] * 2,
+        out_specs=pl.BlockSpec(memory_space=pltpu.VMEM),
+        scratch_shapes=[
+            pltpu.VMEM((slots, size, size), f32),
+            pltpu.VMEM((block, n_ab * block, n_ab * size), bf16),
+            pltpu.VMEM((block, n_ab * block, n_ab * size), bf16),
+            pltpu.VMEM((n_ab, occ_dev, size), f32),
+            pltpu.VMEM((LANES, n_ab * size), bf16),
+            pltpu.VMEM((LANES, n_ab * size), bf16),
+            pltpu.VMEM((chunks, n_cd, rows, LANES), f32),
+            pltpu.VMEM((chunks, n_cd, rows, LANES), f32),
+            pltpu.VMEM((chunks, rows, LANES), f32),
+            pltpu.VMEM((chunks, targets * piece, LANES), f32),
+            pltpu.VMEM((chunks, targets * piece, LANES), f32),
+            dma((slots,)),
+            dma,
+            dma((chunks, n_ab)),
+            dma((chunks, n_ab)),
+            dma((chunks, n_cd)),
+            dma((chunks, n_cd)),
+            dma((chunks, targets)),
+            dma((chunks, targets)),
+        ],
+        compiler_params=pltpu.CompilerParams(
+            collective_id=0, has_side_effects=True, vmem_limit_bytes=48 * 1024 * 1024
+        ),
+    )(tile_row, tile_col, tile_count, amplitudes, integrals)
+    return jnp.transpose(out, (2, 0, 1))[:, None]
 
 
 def from_partner(block, axis, bit):
@@ -24,7 +233,7 @@
     return placed.reshape(width // block_size, occ_dev, row_picks.shape[0] * block_size)
 
 
-def per_device(amplitudes, integrals, tile_row, tile_col, tile_count):
+def general(amplitudes, integrals, tile_row, tile_col, tile_count):
     occ_dev = amplitudes.shape[0]
     slots = integrals.shape[0]
     tile_size = integrals.shape[1]
@@ -60,6 +269,18 @@
     return (direct + partner).reshape(occ_dev, 1, group_size, blocks * block_size)
 
 
+def per_device(amplitudes, integrals, tile_row, tile_col, tile_count):
+    n_ab = lax.axis_size("ab")
+    if (
+        amplitudes.shape[1] == integrals.shape[1]
+        and integrals.shape[0] == n_ab * n_ab
+        and lax.axis_size("ij") == 2
+        and amplitudes.shape[0] % LANES == 0
+    ):
+        return fused(amplitudes, integrals, tile_row, tile_col, tile_count)
+    return general(amplitudes, integrals, tile_row, tile_col, tile_count)
+
+
 def solution(mesh):
     in_specs = (
         P("ij", ("cd", "ab")),

time: 150 us -> 55.8 us (0.37)
  waiting for transfers between devices: 55.6 us -> 0 us
  Pallas kernels: 0 us -> 49.8 us
  local copies, waits for them, and re-layouts: 45.3 us -> 5.15 us
  matrix products: 16.2 us -> 0 us
  between operations: 14.1 us -> 0.67 us
  blocking collectives: 13.3 us -> 0 us
  other arithmetic: 2.69 us -> 0 us
  starting transfers between devices: 2.32 us -> 0 us
    pallas_call x0 -> x1, Pallas kernels: none -> 49.8 us  [fused(): pl.pallas_call(functools.partial(ladder_kernel, n_ab, n_cd, block, chunks...]
    all_gather x1 -> x0, waiting for transfers between devices: 27.2 us -> none  [per_device(): gathered = lax.all_gather(amplitudes, 'ab', axis=1, tiled=True)]
    reduce_scatter x1 -> x0, waiting for transfers between devices: 27.2 us -> none  [per_device(): lax.psum_scatter(partial_value, 'cd', scatter_dimension=0, tiled=True)]
    reshape x5 -> x0, local copies, waits for them, and re-layouts: 21.4 us -> none  [the longest x1 12.9 us: per_device(): arrived = arrived.reshape(blocks, cd_size, occ_dev, group_size, group_size)]
    dot_general x2 -> x0, matrix products: 16.2 us -> none  [the longest x1 12.3 us: place_rows(): jnp.einsum('okf,kef->oke', chosen, tile_rows, precision=lax.Precision.HIG...]
    all_to_all x1 -> x0, blocking collectives: 13.3 us -> none  [per_device(): lax.all_to_all(outgoing.reshape(blocks * cd_size, occ_dev * group_size *...]
    all_to_all x1 -> x0, local copies, waits for them, and re-layouts: 11.3 us -> none  [per_device(): lax.all_to_all(outgoing.reshape(blocks * cd_size, occ_dev * group_size *...]
    transpose x2 -> x0, local copies, waits for them, and re-layouts: 8.03 us -> none  [the longest x1 6.88 us: per_device(): jnp.transpose(arrived, (2, 4, 0, 1, 3))]
  transfers between devices with their start and end apart: 3 -> 0, of which waited for: 3 -> 0; matrix products, arithmetic and copies ran while one was open for 1% -> 0% of each run, Pallas kernels for 0% -> 0%
where the time goes in v1:
time: 55.8 us; the launch traced here: 55.6 us
  Pallas kernels  49.8 us (89%)
  local copies, waits for them, and re-layouts  5.15 us (9%)
  between operations  0.67 us (1%)
    pallas_call x1, Pallas kernels, fused(): pl.pallas_call(functools.partial(ladder_kernel, n_ab, n_cd, block, chunks...  49.8 us
    unnamed x9, local copies, waits for them, and re-layouts  5.15 us

profile of v1, /device:TPU:1, one launch (start us, length us, event | category | flops | bytes accessed | tf_op | source)
XLA Modules:
  0.0 55.6 jit_solution(2249094997690095606)
XLA Ops:
  0.7 0.0 copy-start
  0.7 2.2 %copy-done = f32[16,256,256]{2,1,0:T(8,128)S(1)} copy-done((f32[16,256,256]{2,1,0:T(8,128)S(1)}, f32[16,256,256]{2,1,0:T(8,128)}, u32[]{:S(2)}) %copy-start) | copy-done | bytes 4194328
  2.8 0.0 copy-start.1
  2.8 0.9 %copy-done.1 = f32[256,256]{1,0:T(8,128)S(1)} copy-done((f32[256,256]{1,0:T(8,128)S(1)}, f32[256,256]{1,0:T(8,128)}, u32[]{:S(2)}) %copy-start.1) | copy-done | bytes 262168
  3.8 0.0 copy-start.2
  3.8 0.7 %copy-done.2 = s32[16]{0:T(128)S(1)} copy-done((s32[16]{0:T(128)S(1)}, s32[16]{0:T(128)}, u32[]{:S(2)}) %copy-start.2) | copy-done | bytes 88
  4.4 0.0 copy-start.3
  4.4 0.7 %copy-done.3 = s32[16]{0:T(128)S(1)} copy-done((s32[16]{0:T(128)S(1)}, s32[16]{0:T(128)}, u32[]{:S(2)}) %copy-start.3) | copy-done | bytes 88
  5.1 49.8 %shard_map.55 = f32[4,64,256]{2,1,0:T(8,128)S(1)} custom-call(s32[16]{0:T(128)S(1)} %copy-done.2, s32[16]{0:T(128)S(1)} %copy-done.3, s32[1]{0:T(128)S(6)} %copy.7.count_ref, f32[256,256]{1,0:T(8,128)S(1)} %copy-done.1, f32[16,256,256]{2,1,0:T(8,128)S(1)} %copy-done), custom_call_target="tpu_custom_call" | custom-call | tf_op jit(solution)/shard_map/pallas_call | solution.py:184
  54.9 0.7 %copy.8 = f32[256,1,4,64]{0,3,2,1:T(8,128)} copy(f32[256,1,4,64]{0,3,2,1:T(8,128)S(1)} %bitcast.3) | data formatting | bytes 524288
Async XLA Ops:
  0.7 2.2 %copy-start = (f32[16,256,256]{2,1,0:T(8,128)S(1)}, f32[16,256,256]{2,1,0:T(8,128)}, u32[]{:S(2)}) copy-start(f32[16,256,256]{2,1,0:T(8,128)} %tiles_ref.1) | copy-start | bytes 12582916
  2.8 0.9 %copy-start.1 = (f32[256,256]{1,0:T(8,128)S(1)}, f32[256,256]{1,0:T(8,128)}, u32[]{:S(2)}) copy-start(f32[256,256]{1,0:T(8,128)} %amp_ref.1) | copy-start | bytes 786436
  3.8 0.7 %copy-start.2 = (s32[16]{0:T(128)S(1)}, s32[16]{0:T(128)}, u32[]{:S(2)}) copy-start(s32[16]{0:T(128)} %row_ref.1) | copy-start | bytes 196
  4.4 0.7 %copy-start.3 = (s32[16]{0:T(128)S(1)}, s32[16]{0:T(128)}, u32[]{:S(2)}) copy-start(s32[16]{0:T(128)} %col_ref.1) | copy-start | bytes 196

commit v2 on v1

--- a/solution.py
+++ b/solution.py
@@ -10,6 +10,7 @@
 
 MESH = pl.DeviceIdType.MESH
 LANES = 128
+VMEM_BYTES = 63 * 1024 * 1024
 
 
 def split(value):
@@ -21,8 +22,10 @@
 def ladder_kernel(
     n_ab, n_cd, block, chunks,
     row_ref, col_ref, count_ref, amp_ref, tiles_ref, out_ref,
-    tiles, w_high, w_low, gathered, a_high, a_low, partial, arrived, summed, outgoing, mirrored,
-    tile_sem, own_sem, ag_send, ag_recv, rs_send, rs_recv, mi_send, mi_recv,
+    tiles, w_high, w_low, gathered, a_high, a_low, partial, up_in, down_in, up_out, down_out,
+    summed, outgoing, mirrored,
+    tile_sem, own_sem, ag_send, ag_recv, up_send, up_recv, down_send, down_recv,
+    mi_send, mi_recv,
 ):
     me_ab, me_cd, me_ij = lax.axis_index("ab"), lax.axis_index("cd"), lax.axis_index("ij")
     slots, size = tiles_ref.shape[0], tiles_ref.shape[1]
@@ -85,17 +88,94 @@
             w_low[at] = low.reshape(block, block, size)
 
     own.wait()
-    rs = {}
     mi = {}
     contract = (((1,), (1,)), ((), ()))
+    last = n_cd - 1
+
+    def up(h, d, source):
+        return pltpu.make_async_remote_copy(
+            src_ref=source.at[h, d],
+            dst_ref=up_in.at[h, d],
+            send_sem=up_send.at[h, d],
+            recv_sem=up_recv.at[h, d],
+            device_id=(me_ab, me_cd + 1, me_ij),
+            device_id_type=MESH,
+        )
+
+    def down(h, d, source):
+        return pltpu.make_async_remote_copy(
+            src_ref=source.at[h, d],
+            dst_ref=down_in.at[h, d],
+            send_sem=down_send.at[h, d],
+            recv_sem=down_recv.at[h, d],
+            device_id=(me_ab, me_cd - 1, me_ij),
+            device_id_type=MESH,
+        )
+
+    def compute(h):
+        part = pl.ds(h * LANES, LANES)
+        for j in range(n_ab):
+            if j:
+                ag[h, j].wait_recv()
+            high, low = split(gathered[j, part])
+            a_high[:, pl.ds(j * size, size)] = high
+            a_low[:, pl.ds(j * size, size)] = low
+        for i in range(n_cd):
+            d = jnp.where(me_cd < n_cd // 2, last - i, i)
+            lead = pl.ds(d * group, group)
+            left_high = w_high[lead].reshape(rows, n_ab * size)
+            left_low = w_low[lead].reshape(rows, n_ab * size)
+            right_high, right_low = a_high[...], a_low[...]
+            value = lax.dot_general(
+                left_high, right_low, contract, preferred_element_type=jnp.float32
+            )
+            value += lax.dot_general(
+                left_low, right_high, contract, preferred_element_type=jnp.float32
+            )
+            value += lax.dot_general(
+                left_high, right_high, contract, preferred_element_type=jnp.float32
+            )
+            partial[h, d] = value
+            if i < last:
+
+                @pl.when(me_cd == 0)
+                def _():
+                    up(h, d, partial).start()
+
+                @pl.when(me_cd == last)
+                def _():
+                    down(h, d, partial).start()
+
+    def relay(h, step):
+        for_up = last + me_cd - step
+
+        @pl.when((me_cd >= 1) & (me_cd <= step))
+        def _():
+            up(h, for_up, up_out).wait_recv()
+            if step < last:
+                up_out[h, for_up] = partial[h, for_up] + up_in[h, for_up]
+                up(h, for_up, up_out).start()
+
+        for_down = step - last + me_cd
+
+        @pl.when((me_cd < last) & (for_down >= 0))
+        def _():
+            down(h, for_down, down_out).wait_recv()
+            if step < last:
+                down_out[h, for_down] = partial[h, for_down] + down_in[h, for_down]
+                down(h, for_down, down_out).start()
 
     def finish(h):
-        for i in range(1, n_cd):
-            rs[h, i].wait_recv()
-        total = partial[h, 0]
-        for i in range(1, n_cd):
-            total = total + arrived[h, i]
-        summed[h] = total
+        summed[h] = partial[h, me_cd]
+
+        @pl.when(me_cd > 0)
+        def _():
+            summed[h] += up_in[h, me_cd]
+
+        @pl.when(me_cd < last)
+        def _():
+            summed[h] += down_in[h, me_cd]
+
         for x in range(group):
             for y in range(group):
                 outgoing[h, pl.ds(x * group + y, targets, stride=piece), :] = summed[
@@ -114,42 +194,18 @@
                 )
                 mi[h, t].start()
 
+    waiting = None
     for h in range(chunks):
-        part = pl.ds(h * LANES, LANES)
-        for j in range(n_ab):
-            if j:
-                ag[h, j].wait_recv()
-            high, low = split(gathered[j, part])
-            a_high[:, pl.ds(j * size, size)] = high
-            a_low[:, pl.ds(j * size, size)] = low
-        for i in [*range(1, n_cd), 0]:
-            d = lax.rem(me_cd + i, n_cd)
-            lead = pl.ds(d * group, group)
-            left_high = w_high[lead].reshape(rows, n_ab * size)
-            left_low = w_low[lead].reshape(rows, n_ab * size)
-            right_high, right_low = a_high[...], a_low[...]
-            value = lax.dot_general(
-                left_high, right_low, contract, preferred_element_type=jnp.float32
-            )
-            value += lax.dot_general(
-                left_low, right_high, contract, preferred_element_type=jnp.float32
-            )
-            value += lax.dot_general(
-                left_high, right_high, contract, preferred_element_type=jnp.float32
-            )
-            partial[h, i] = value
-            if i:
-                rs[h, i] = pltpu.make_async_remote_copy(
-                    src_ref=partial.at[h, i],
-                    dst_ref=arrived.at[h, i],
-                    send_sem=rs_send.at[h, i],
-                    recv_sem=rs_recv.at[h, i],
-                    device_id=(me_ab, d, me_ij),
-                    device_id_type=MESH,
-                )
-                rs[h, i].start()
-    for h in range(chunks):
-        finish(h)
+        compute(h)
+        if waiting is not None:
+            for step in range(2, n_cd):
+                relay(waiting, step)
+            finish(waiting)
+        relay(h, 1)
+        waiting = h
+    for step in range(2, n_cd):
+        relay(waiting, step)
+    finish(waiting)
     for h in range(chunks):
         for s in range(targets):
             pltpu.make_async_remote_copy(
@@ -165,7 +221,18 @@
                 summed[h, pl.ds(y * n_ab * block, n_ab * block), :]
                 + mirrored[h, pl.ds(y, targets * group, stride=group), :]
             )
-    for copy in [*ag.values(), *rs.values(), *mi.values()]:
+    for h in range(chunks):
+        for d in range(n_cd):
+
+            @pl.when(me_cd < d)
+            def _():
+                up(h, d, up_out).wait_send()
+
+            @pl.when(me_cd > d)
+            def _():
+                down(h, d, down_out).wait_send()
+
+    for copy in [*ag.values(), *mi.values()]:
         copy.wait_send()
 
 
@@ -194,8 +261,7 @@
             pltpu.VMEM((n_ab, occ_dev, size), f32),
             pltpu.VMEM((LANES, n_ab * size), bf16),
             pltpu.VMEM((LANES, n_ab * size), bf16),
-            pltpu.VMEM((chunks, n_cd, rows, LANES), f32),
-            pltpu.VMEM((chunks, n_cd, rows, LANES), f32),
+            *[pltpu.VMEM((chunks, n_cd, rows, LANES), f32)] * 5,
             pltpu.VMEM((chunks, rows, LANES), f32),
             pltpu.VMEM((chunks, targets * piece, LANES), f32),
             pltpu.VMEM((chunks, targets * piece, LANES), f32),
@@ -203,13 +269,12 @@
             dma,
             dma((chunks, n_ab)),
             dma((chunks, n_ab)),
-            dma((chunks, n_cd)),
-            dma((chunks, n_cd)),
+            *[dma((chunks, n_cd))] * 4,
             dma((chunks, targets)),
             dma((chunks, targets)),
         ],
         compiler_params=pltpu.CompilerParams(
-            collective_id=0, has_side_effects=True, vmem_limit_bytes=48 * 1024 * 1024
+            collective_id=0, has_side_effects=True, vmem_limit_bytes=VMEM_BYTES
         ),
     )(tile_row, tile_col, tile_count, amplitudes, integrals)
     return jnp.transpose(out, (2, 0, 1))[:, None]

time: 55.8 us -> 48.9 us (0.88)
  local copies, waits for them, and re-layouts: 5.15 us -> 1.67 us
  Pallas kernels: 49.8 us -> 46.4 us
    unnamed x9 -> x1, local copies, waits for them, and re-layouts: 5.15 us -> 1.67 us
    pallas_call x1, Pallas kernels: 49.8 us -> 46.4 us  [fused(): pl.pallas_call(functools.partial(ladder_kernel, n_ab, n_cd, block, chunks...]
where the time goes in v2:
time: 48.9 us; the launch traced here: 48.8 us
  Pallas kernels  46.4 us (95%)
  local copies, waits for them, and re-layouts  1.67 us (3%)
  between operations  0.66 us (1%)
    pallas_call x1, Pallas kernels, fused(): pl.pallas_call(functools.partial(ladder_kernel, n_ab, n_cd, block, chunks...  46.4 us
    unnamed x1, local copies, waits for them, and re-layouts  1.67 us

profile of v2, /device:TPU:1, one launch (start us, length us, event | category | flops | bytes accessed | tf_op | source)
XLA Modules:
  0.0 48.8 jit_solution(16473711224422871199)
XLA Ops:
  0.7 46.4 %shard_map.55 = f32[4,64,256]{2,1,0:T(8,128)} custom-call(s32[16]{0:T(128)} %row_ref.1, s32[16]{0:T(128)} %col_ref.1, s32[1]{0:T(128)S(6)} %copy.7.count_ref, f32[256,256]{1,0:T(8,128)} %amp_ref.1, f32[16,256,256]{2,1,0:T(8,128)} %tiles_ref.1), custom_call_target="tpu_custom_call" | custom-call | tf_op jit(solution)/shard_map/pallas_call | solution.py:251
  47.1 1.7 %copy.8 = f32[256,1,4,64]{0,3,2,1:T(8,128)} copy(f32[256,1,4,64]{0,3,2,1:T(8,128)} %bitcast.3) | data formatting | bytes 524288

commit v3 on v2

--- a/solution.py
+++ b/solution.py
@@ -48,14 +48,18 @@
         pl.semaphore_signal(
             barrier, inc=1, device_id=(lax.rem(me_ab + j, n_ab), me_cd, me_ij), device_id_type=MESH
         )
-    for i in range(1, n_cd):
-        pl.semaphore_signal(
-            barrier, inc=1, device_id=(me_ab, lax.rem(me_cd + i, n_cd), me_ij), device_id_type=MESH
-        )
-    for p in range(n_ab):
-        for q in range(n_cd):
-            pl.semaphore_signal(barrier, inc=1, device_id=(p, q, 1 - me_ij), device_id_type=MESH)
-    pl.semaphore_wait(barrier, n_ab - 1 + n_cd - 1 + targets)
+    pl.semaphore_signal(barrier, inc=1, device_id=(me_ab, me_cd, 1 - me_ij), device_id_type=MESH)
+
+    @pl.when(me_cd > 0)
+    def _():
+        pl.semaphore_signal(barrier, inc=1, device_id=(me_ab, me_cd - 1, me_ij), device_id_type=MESH)
+
+    @pl.when(me_cd < n_cd - 1)
+    def _():
+        pl.semaphore_signal(barrier, inc=1, device_id=(me_ab, me_cd + 1, me_ij), device_id_type=MESH)
+
+    ends = jnp.where(me_cd > 0, 1, 0) + jnp.where(me_cd < n_cd - 1, 1, 0)
+    pl.semaphore_wait(barrier, n_ab + ends)
 
     ag = {}
     for h in range(chunks):
@@ -181,10 +185,12 @@
                 outgoing[h, pl.ds(x * group + y, targets, stride=piece), :] = summed[
                     h, pl.ds(x * n_ab * block + y, targets, stride=group), :
                 ]
-        for p in range(n_ab):
-            for q in range(n_cd):
+        for i in range(n_cd):
+            q = jnp.where(me_cd < n_cd // 2, last - i, i)
+            for j in range(n_ab):
+                p = lax.rem(me_ab + j, n_ab)
                 t = p * n_cd + q
-                mi[h, t] = pltpu.make_async_remote_copy(
+                mi[h, i, j] = pltpu.make_async_remote_copy(
                     src_ref=outgoing.at[h, pl.ds(t * piece, piece)],
                     dst_ref=mirrored.at[h, pl.ds(own_place * piece, piece)],
                     send_sem=mi_send.at[h, t],
@@ -192,7 +198,7 @@
                     device_id=(p, q, 1 - me_ij),
                     device_id_type=MESH,
                 )
-                mi[h, t].start()
+                mi[h, i, j].start()
 
     waiting = None
     for h in range(chunks):

time: 48.9 us -> 48.9 us (level)
  no operation moved by 1% of the time
where the time goes in v3:
time: 48.9 us; the launch traced here: 48.7 us
  Pallas kernels  46.4 us (95%)
  local copies, waits for them, and re-layouts  1.67 us (3%)
  between operations  0.66 us (1%)
    pallas_call x1, Pallas kernels, fused(): pl.pallas_call(functools.partial(ladder_kernel, n_ab, n_cd, block, chunks...  46.4 us
    unnamed x1, local copies, waits for them, and re-layouts  1.67 us

profile of v3, /device:TPU:1, one launch (start us, length us, event | category | flops | bytes accessed | tf_op | source)
XLA Modules:
  0.0 48.7 jit_solution(321398600271161330)
XLA Ops:
  0.7 46.4 %shard_map.55 = f32[4,64,256]{2,1,0:T(8,128)} custom-call(s32[16]{0:T(128)} %row_ref.1, s32[16]{0:T(128)} %col_ref.1, s32[1]{0:T(128)S(6)} %copy.7.count_ref, f32[256,256]{1,0:T(8,128)} %amp_ref.1, f32[16,256,256]{2,1,0:T(8,128)} %tiles_ref.1), custom_call_target="tpu_custom_call" | custom-call | tf_op jit(solution)/shard_map/pallas_call | solution.py:257
  47.0 1.7 %copy.8 = f32[256,1,4,64]{0,3,2,1:T(8,128)} copy(f32[256,1,4,64]{0,3,2,1:T(8,128)} %bitcast.3) | data formatting | bytes 524288

commit v4 on v3

--- a/solution.py
+++ b/solution.py
@@ -22,7 +22,7 @@
 def ladder_kernel(
     n_ab, n_cd, block, chunks,
     row_ref, col_ref, count_ref, amp_ref, tiles_ref, out_ref,
-    tiles, w_high, w_low, gathered, a_high, a_low, partial, up_in, down_in, up_out, down_out,
+    tiles, w_high, w_low, gathered, a_both, partial, up_in, down_in, up_out, down_out,
     summed, outgoing, mirrored,
     tile_sem, own_sem, ag_send, ag_recv, up_send, up_recv, down_send, down_recv,
     mi_send, mi_recv,
@@ -73,7 +73,8 @@
                 device_id=(lax.rem(me_ab + j, n_ab), me_cd, me_ij),
                 device_id_type=MESH,
             )
-            ag[h, j].start()
+            if h == 0:
+                ag[h, j].start()
 
     keys = [row_ref[k] * n_ab + col_ref[k] for k in range(slots)]
     live_count = count_ref[0]
@@ -121,24 +122,22 @@
         for j in range(n_ab):
             if j:
                 ag[h, j].wait_recv()
+                if h + 1 < chunks:
+                    ag[h + 1, j].start()
             high, low = split(gathered[j, part])
-            a_high[:, pl.ds(j * size, size)] = high
-            a_low[:, pl.ds(j * size, size)] = low
+            a_both[pl.ds(0, LANES), pl.ds(j * size, size)] = high
+            a_both[pl.ds(LANES, LANES), pl.ds(j * size, size)] = low
         for i in range(n_cd):
             d = jnp.where(me_cd < n_cd // 2, last - i, i)
             lead = pl.ds(d * group, group)
             left_high = w_high[lead].reshape(rows, n_ab * size)
             left_low = w_low[lead].reshape(rows, n_ab * size)
-            right_high, right_low = a_high[...], a_low[...]
-            value = lax.dot_general(
-                left_high, right_low, contract, preferred_element_type=jnp.float32
+            right = a_both[...]
+            wide = lax.dot_general(left_high, right, contract, preferred_element_type=jnp.float32)
+            value = wide[:, LANES:] + lax.dot_general(
+                left_low, right[:LANES], contract, preferred_element_type=jnp.float32
             )
-            value += lax.dot_general(
-                left_low, right_high, contract, preferred_element_type=jnp.float32
-            )
-            value += lax.dot_general(
-                left_high, right_high, contract, preferred_element_type=jnp.float32
-            )
+            value += wide[:, :LANES]
             partial[h, d] = value
             if i < last:
 
@@ -265,8 +264,7 @@
             pltpu.VMEM((block, n_ab * block, n_ab * size), bf16),
             pltpu.VMEM((block, n_ab * block, n_ab * size), bf16),
             pltpu.VMEM((n_ab, occ_dev, size), f32),
-            pltpu.VMEM((LANES, n_ab * size), bf16),
-            pltpu.VMEM((LANES, n_ab * size), bf16),
+            pltpu.VMEM((2 * LANES, n_ab * size), bf16),
             *[pltpu.VMEM((chunks, n_cd, rows, LANES), f32)] * 5,
             pltpu.VMEM((chunks, rows, LANES), f32),
             pltpu.VMEM((chunks, targets * piece, LANES), f32),

time: 48.9 us -> 47.7 us (0.975)
  Pallas kernels: 46.4 us -> 45.2 us
    pallas_call x1, Pallas kernels: 46.4 us -> 45.2 us  [fused(): pl.pallas_call(functools.partial(ladder_kernel, n_ab, n_cd, block, chunks...]
where the time goes in v4:
time: 47.7 us; the launch traced here: 47.5 us
  Pallas kernels  45.2 us (95%)
  local copies, waits for them, and re-layouts  1.67 us (4%)
  between operations  0.66 us (1%)
    pallas_call x1, Pallas kernels, fused(): pl.pallas_call(functools.partial(ladder_kernel, n_ab, n_cd, block, chunks...  45.2 us
    unnamed x1, local copies, waits for them, and re-layouts  1.67 us

profile of v4, /device:TPU:1, one launch (start us, length us, event | category | flops | bytes accessed | tf_op | source)
XLA Modules:
  0.0 47.5 jit_solution(1092443357457127831)
XLA Ops:
  0.7 45.2 %shard_map.55 = f32[4,64,256]{2,1,0:T(8,128)} custom-call(s32[16]{0:T(128)} %row_ref.1, s32[16]{0:T(128)} %col_ref.1, s32[1]{0:T(128)S(6)} %copy.7.count_ref, f32[256,256]{1,0:T(8,128)} %amp_ref.1, f32[16,256,256]{2,1,0:T(8,128)} %tiles_ref.1), custom_call_target="tpu_custom_call" | custom-call | tf_op jit(solution)/shard_map/pallas_call | solution.py:256
  45.8 1.7 %copy.8 = f32[256,1,4,64]{0,3,2,1:T(8,128)} copy(f32[256,1,4,64]{0,3,2,1:T(8,128)} %bitcast.3) | data formatting | bytes 524288
